TPU v7x, 32 devices: a whole 2x2x4 slice. The times are simulated.
32 devices in a mesh: grp: 2 (over core), tm: 16 (over z, y, x).
Axes of the slice: x: 2, y: 2, z: 4, core: 2. Of those that a mesh axis runs over, the one named last changes fastest.
Arguments:
- x_start: float32 [512, 128], P(('grp', 'tm')), may hold values from -3 to 3
- y_start: float32 [512, 128], P('tm'), may hold values from 0 to 1
- cost: float32 [512, 128], P(('grp', 'tm')), may hold values from -6 to 6
- rhs: float32 [512, 128], P('tm'), may hold values from -6 to 6
- tiles: float32 [2048, 128, 128], P(('grp', 'tm')), may hold values from -0.375 to 0.375
- tile_rows: int32 [2048], P(('grp', 'tm')), may hold values from 0 to 511, as said below
- tile_cols: int32 [2048], P(('grp', 'tm')), may hold values from 0 to 511, as said below
- tile_count: int32 [32], P(('grp', 'tm')), may hold values from 1 to 64, as said below
- var_class: int32 [512, 128], P(('grp', 'tm')), may hold values from 0 to 7
- lower_table: float32 [8], replicated, may hold values from -1 to -0.2
- upper_table: float32 [8], replicated, may hold values from 0.2 to 1
Outputs:
- primal: float32 [512, 128], P(('grp', 'tm'))
- dual: float32 [512, 128], P('tm')
- primal_mean: float32 [512, 128], P(('grp', 'tm'))
- dual_mean: float32 [512, 128], P('tm')
Inputs may be any that keep to these rules, and one draw needn't show every extreme that they name: `tile_cols`: the tile slots of device d (slots d * 64 to (d + 1) * 64 - 1) name only that device's own column blocks d * 16 to (d + 1) * 16 - 1. `tile_rows`: the tile slots of device d = g * 16 + t name only row blocks of time blocks t - 1, t and t + 1 (rows k * 32 to (k + 1) * 32 - 1 belong to time block k). Only the first tile_count[d] slots of device d are live; some device has all 64 slots live.
All inputs are finite; a program needn't handle non-finite values.
Results may differ from a plain program's by a relative error of at most 0.0001.
Values sent between devices are 32-bit elements; how exact they have to be, the bound alone decides.
No kernel may reach another device: no remote copies, remote signals or barrier semaphores. Data moves between devices by JAX's collectives and lax.ppermute only.
A program may use at most 64 MiB of HBM per device.

v0:
```python
import jax
import jax.numpy as jnp
from jax import lax
from jax.sharding import PartitionSpec as P

ITERS = 2
primal_step = 0.6
dual_step = 0.6


def with_halo(block, sides, width):
    for axis, dim in sides:
        count = lax.axis_size(axis)
        forward = [(i, i + 1) for i in range(count - 1)]
        backward = [(target, source) for source, target in forward]
        low = lax.ppermute(
            lax.slice_in_dim(block, block.shape[dim] - width, None, axis=dim), axis, forward
        )
        high = lax.ppermute(lax.slice_in_dim(block, 0, width, axis=dim), axis, backward)
        block = jnp.concatenate([low, block, high], axis=dim)
    return block


def shifted(block, axis, distance):
    devices = range(lax.axis_size(axis))
    route = [(i - distance, i) for i in devices if i - distance in devices]
    return lax.ppermute(block, axis, route)


def dual_update(dual_part, rhs_part, image_part):
    return jnp.maximum(dual_part + dual_step * (rhs_part - image_part), 0.0)


def body(
    x_start,
    y_start,
    cost,
    rhs,
    tiles,
    tile_rows,
    tile_cols,
    tile_count,
    var_class,
    lower_table,
    upper_table,
):
    tile_total = tiles.shape[0]
    col_blocks = x_start.shape[0]
    row_blocks = y_start.shape[0]
    time_devices = lax.axis_size("tm")
    time_index = lax.axis_index("tm")
    device_index = lax.axis_index("grp") * time_devices + time_index
    local_cols = tile_cols - device_index * col_blocks
    live_mask = (jnp.arange(tile_total) < tile_count[0]).astype(jnp.float32)[:, None]
    col_select = (local_cols[:, None] == jnp.arange(col_blocks)[None, :]).astype(jnp.float32)
    lower_bound = jnp.zeros(x_start.shape, jnp.float32)
    upper_bound = jnp.zeros(x_start.shape, jnp.float32)
    for class_id in range(lower_table.shape[0]):
        lower_bound = jnp.where(var_class == class_id, lower_table[class_id], lower_bound)
        upper_bound = jnp.where(var_class == class_id, upper_table[class_id], upper_bound)
    window_first = (time_index - 1) * row_blocks
    row_select = (
        (tile_rows - window_first)[:, None] == jnp.arange(3 * row_blocks)[None, :]
    ).astype(jnp.float32)
    dual_view = with_halo(y_start, (("tm", 0),), row_blocks)
    primal = x_start
    dual = y_start
    primal_total = jnp.zeros_like(x_start)
    dual_total = jnp.zeros_like(y_start)
    for iteration in range(ITERS):
        dual_picked = jnp.dot(row_select, dual_view, precision=lax.Precision.HIGHEST)
        backward = (
            jnp.einsum("nrc,nr->nc", tiles, dual_picked, precision=lax.Precision.HIGHEST)
            * live_mask
        )
        adjoint_part = jnp.dot(col_select.T, backward, precision=lax.Precision.HIGHEST)
        moved = primal - primal_step * (cost - adjoint_part)
        primal_next = jnp.minimum(jnp.maximum(moved, lower_bound), upper_bound)
        extrapolated = 2.0 * primal_next - primal
        primal_picked = jnp.dot(col_select, extrapolated, precision=lax.Precision.HIGHEST)
        forward = (
            jnp.einsum("nrc,nc->nr", tiles, primal_picked, precision=lax.Precision.HIGHEST)
            * live_mask
        )
        window_terms = jnp.dot(row_select.T, forward, precision=lax.Precision.HIGHEST)
        summed = lax.psum(window_terms, "grp")
        from_above = shifted(summed[:row_blocks], "tm", -1)
        from_below = shifted(summed[2 * row_blocks :], "tm", 1)
        image_slab = summed[row_blocks : 2 * row_blocks] + from_above + from_below
        dual_next = dual_update(dual, rhs, image_slab)
        if iteration + 1 < ITERS:
            dual_view = with_halo(dual_next, (("tm", 0),), row_blocks)
        primal_total = primal_total + primal_next
        dual_total = dual_total + dual_next
        primal = primal_next
        dual = dual_next
    return (primal, dual, primal_total / ITERS, dual_total / ITERS)


def solution(mesh):
    return jax.shard_map(
        body,
        mesh=mesh,
        in_specs=(
            P(("grp", "tm"), None),
            P("tm", None),
            P(("grp", "tm"), None),
            P("tm", None),
            P(("grp", "tm"), None, None),
            P(("grp", "tm")),
            P(("grp", "tm")),
            P(("grp", "tm")),
            P(("grp", "tm"), None),
            P(),
            P(),
        ),
        out_specs=(P(("grp", "tm"), None), P("tm", None), P(("grp", "tm"), None), P("tm", None)),
        check_vma=False,
    )
```

profile of v0, /device:TPU:16, one launch (start us, length us, event | category | flops | bytes accessed | tf_op | source)
XLA Modules:
  0.0 100.7 jit_solution(15821462959131894350)
XLA Ops:
  0.7 4.4 %collective-permute-start.1 = (f32[32,128]{1,0:T(8,128)}, f32[32,128]{1,0:T(8,128)S(1)}, u32[]{:S(2)}, u32[]{:S(2)}) collective-permute-start(f32[32,128]{1,0:T(8,128)} %param.12), channel_id=1, source_target_pairs={{1,0},{2,1},{3,2},{4,3},{5,4},{6,5},{7,6},{8,7},{9,8},{10,9},{11,1... | collective-permute-start | bytes 49160 | tf_op jit(solution)/shard_map/ppermute | solution.py:19
  5.0 1.9 %collective-permute-start = (f32[32,128]{1,0:T(8,128)}, f32[32,128]{1,0:T(8,128)S(1)}, u32[]{:S(2)}, u32[]{:S(2)}) collective-permute-start(f32[32,128]{1,0:T(8,128)} %param.12), channel_id=1, source_target_pairs={{0,1},{1,2},{2,3},{3,4},{4,5},{5,6},{6,7},{7,8},{8,9},{9,10},{10,1... | collective-permute-start | bytes 49160 | tf_op jit(solution)/shard_map/ppermute | solution.py:16
  7.6 1.6 %fusion.64 = (f32[1]{0:T(128)}, f32[1]{0:T(128)}, f32[1]{0:T(128)}, f32[1]{0:T(128)}, f32[1]{0:T(128)}, /*index=5*/f32[1]{0:T(128)}, f32[1]{0:T(128)}, f32[1]{0:T(128)}) fusion(f32[8]{0:T(128)} %param.20), kind=kLoop, calls=%fused_computation.84 | loop fusion | bytes 64 | tf_op jit(solution)/shard_map/slice | solution.py:59
  9.3 1.6 %fusion.63 = (f32[1]{0:T(128)}, f32[1]{0:T(128)}, f32[1]{0:T(128)}, f32[1]{0:T(128)}, f32[1]{0:T(128)}, /*index=5*/f32[1]{0:T(128)}, f32[1]{0:T(128)}, f32[1]{0:T(128)}) fusion(f32[8]{0:T(128)} %param.21), kind=kLoop, calls=%fused_computation.83 | loop fusion | bytes 64 | tf_op jit(solution)/shard_map/slice | solution.py:60
  11.6 0.8 broadcast_subtract_fusion.1
  12.4 0.8 broadcast_subtract_fusion
  13.3 0.9 fusion.8
  14.2 5.3 %fusion.65 = f32[64,1,128]{2,1,0:T(1,128)S(1)} fusion(f32[64,128,1]{1,2,0:T(1,128)S(1)} %bitcast.46, f32[64,128,128]{2,1,0:T(8,128)} %param.15), kind=kOutput, calls=%fused_computation.85 | convolution fusion | flops 12582912 | bytes 4259840 | tf_op jit(solution)/shard_map/nrc,nr->nc/dot_general | solution.py:73
  19.5 10.4 %fusion.7 = f32[16,128]{1,0:T(8,128)S(1)} fusion(f32[16,128]{1,0:T(8,128)S(1)} %copy-done.4, f32[16,128]{1,0:T(8,128)S(1)} %copy-done.5, f32[64,128]{1,0:T(8,128)S(1)} %bitcast.49, f32[64]{0:T(128)S(1)} %compare_convert_fusion, s32[64]{0:T(128)S(1)} %broadcast_subtract_fusion.1, pred[16,128]{1,0:T(8,128)(4,1)S(1)} %get-tuple-element.16, ...), kind=kOutput, calls=%fused_computation.9 | convolution fusion | flops 1625088 | bytes 74304 | tf_op jit(solution)/shard_map/dot_general | solution.py:76
  30.2 6.6 %fusion.66 = f32[64,1,128]{2,1,0:T(1,128)S(1)} fusion(f32[64,128,1]{1,2,0:T(1,128)S(1)} %bitcast.53, f32[64,128,128]{2,1,0:T(8,128)S(1)} %copy-done), kind=kOutput, calls=%fused_computation.86 | convolution fusion | flops 12582912 | bytes 4259840 | tf_op jit(solution)/shard_map/nrc,nc->nr/dot_general | solution.py:82
  37.1 3.5 %psum.14 = f32[96,128]{1,0:T(8,128)S(1)} all-reduce(f32[96,128]{1,0:T(8,128)S(1)} %fusion.23), channel_id=1, replica_groups=mesh['grp'=2,'tm'=16] {'grp'}, use_global_device_ids=true, to_apply=%region_0.1 | all-reduce | flops 12288 | bytes 98304 | tf_op jit(solution)/shard_map/psum | solution.py:86
  40.7 6.0 %collective-permute-start.2 = (f32[32,128]{1,0:T(8,128)S(1)}, f32[32,128]{1,0:T(8,128)S(1)}, u32[]{:S(2)}, u32[]{:S(2)}) collective-permute-start(f32[32,128]{1,0:T(8,128)S(1)} %get-tuple-element.8), channel_id=1, source_target_pairs={{1,0},{2,1},{3,2},{4,3},{5,4},{6,5},{7,6},{8,7},{9,8},{10,9},{11,1... | collective-permute-start | bytes 49160 | tf_op jit(solution)/shard_map/ppermute | solution.py:27
  46.6 1.9 %collective-permute-start.3 = (f32[32,128]{1,0:T(8,128)S(1)}, f32[32,128]{1,0:T(8,128)S(1)}, u32[]{:S(2)}, u32[]{:S(2)}) collective-permute-start(f32[32,128]{1,0:T(8,128)S(1)} %get-tuple-element.9), channel_id=1, source_target_pairs={{0,1},{1,2},{2,3},{3,4},{4,5},{5,6},{6,7},{7,8},{8,9},{9,10},{10,1... | collective-permute-start | bytes 49160 | tf_op jit(solution)/shard_map/ppermute | solution.py:27
  48.6 5.5 %collective-permute-done.3 = f32[32,128]{1,0:T(8,128)S(1)} collective-permute-done((f32[32,128]{1,0:T(8,128)S(1)}, f32[32,128]{1,0:T(8,128)S(1)}, u32[]{:S(2)}, u32[]{:S(2)}) %collective-permute-start.3) | collective-permute-done | bytes 16416 | tf_op jit(solution)/shard_map/ppermute | solution.py:27
  54.1 1.9 %collective-permute-start.5 = (f32[32,128]{1,0:T(8,128)S(1)}, f32[32,128]{1,0:T(8,128)S(1)}, u32[]{:S(2)}, u32[]{:S(2)}) collective-permute-start(f32[32,128]{1,0:T(8,128)S(1)} %fusion.37), channel_id=1, source_target_pairs={{1,0},{2,1},{3,2},{4,3},{5,4},{6,5},{7,6},{8,7},{9,8},{10,9},{11,1... | collective-permute-start | bytes 49160 | tf_op jit(solution)/shard_map/ppermute | solution.py:19
  56.0 4.1 %collective-permute-start.4 = (f32[32,128]{1,0:T(8,128)S(1)}, f32[32,128]{1,0:T(8,128)S(1)}, u32[]{:S(2)}, u32[]{:S(2)}) collective-permute-start(f32[32,128]{1,0:T(8,128)S(1)} %fusion.37), channel_id=1, source_target_pairs={{0,1},{1,2},{2,3},{3,4},{4,5},{5,6},{6,7},{7,8},{8,9},{9,10},{10,1... | collective-permute-start | bytes 49160 | tf_op jit(solution)/shard_map/ppermute | solution.py:16
  60.1 3.3 %collective-permute-done.4 = f32[32,128]{1,0:T(8,128)S(1)} collective-permute-done((f32[32,128]{1,0:T(8,128)S(1)}, f32[32,128]{1,0:T(8,128)S(1)}, u32[]{:S(2)}, u32[]{:S(2)}) %collective-permute-start.4) | collective-permute-done | bytes 16416 | tf_op jit(solution)/shard_map/ppermute | solution.py:16
  63.7 5.3 %fusion.67 = f32[64,1,128]{2,1,0:T(1,128)S(1)} fusion(f32[64,128,1]{1,2,0:T(1,128)S(1)} %bitcast.47, f32[64,128,128]{2,1,0:T(8,128)} %param.15), kind=kOutput, calls=%fused_computation.87 | convolution fusion | flops 12582912 | bytes 4259840 | tf_op jit(solution)/shard_map/nrc,nr->nc/dot_general | solution.py:73
  68.9 11.1 %add_multiply_fusion.1 = (f32[16,128]{1,0:T(8,128)}, f32[16,128]{1,0:T(8,128)S(1)}) fusion(f32[16,128]{1,0:T(8,128)S(1)} %fusion.7, pred[16,128]{1,0:T(8,128)(4,1)S(1)} %get-tuple-element.16, pred[16,128]{1,0:T(8,128)(4,1)S(1)} %get-tuple-element.15, pred[16,128]{1,0:T(8,128)(4,1)S(1)} %get-tuple-element.14, pred[16,128]{1,0:T(8,128)(4,1)S(1)} %get-tuple-element.13, ...), kind=kOutput, calls=%fused_computation.57 | convolution fusion | flops 1629184 | bytes 82496 | tf_op jit(solution)/shard_map/dot_general | solution.py:76
  80.2 6.6 %fusion.68 = f32[64,1,128]{2,1,0:T(1,128)S(1)} fusion(f32[64,128,1]{1,2,0:T(1,128)S(1)} %bitcast.51, f32[64,128,128]{2,1,0:T(8,128)S(1)} %copy-done.1), kind=kOutput, calls=%fused_computation.88 | convolution fusion | flops 12582912 | bytes 4259840 | tf_op jit(solution)/shard_map/nrc,nc->nr/dot_general | solution.py:82
  87.1 3.5 %psum.15 = f32[96,128]{1,0:T(8,128)S(1)} all-reduce(f32[96,128]{1,0:T(8,128)S(1)} %fusion.20), channel_id=1, replica_groups=mesh['grp'=2,'tm'=16] {'grp'}, use_global_device_ids=true, to_apply=%region_1.2 | all-reduce | flops 12288 | bytes 98304 | tf_op jit(solution)/shard_map/psum | solution.py:86
  90.7 1.9 %collective-permute-start.6 = (f32[32,128]{1,0:T(8,128)S(1)}, f32[32,128]{1,0:T(8,128)S(1)}, u32[]{:S(2)}, u32[]{:S(2)}) collective-permute-start(f32[32,128]{1,0:T(8,128)S(1)} %get-tuple-element.6), channel_id=1, source_target_pairs={{1,0},{2,1},{3,2},{4,3},{5,4},{6,5},{7,6},{8,7},{9,8},{10,9},{11,1... | collective-permute-start | bytes 49160 | tf_op jit(solution)/shard_map/ppermute | solution.py:27
  92.6 3.9 %collective-permute-start.7 = (f32[32,128]{1,0:T(8,128)S(1)}, f32[32,128]{1,0:T(8,128)S(1)}, u32[]{:S(2)}, u32[]{:S(2)}) collective-permute-start(f32[32,128]{1,0:T(8,128)S(1)} %get-tuple-element.7), channel_id=1, source_target_pairs={{0,1},{1,2},{2,3},{3,4},{4,5},{5,6},{6,7},{7,8},{8,9},{9,10},{10,1... | collective-permute-start | bytes 49160 | tf_op jit(solution)/shard_map/ppermute | solution.py:27
  96.6 3.5 %collective-permute-done.7 = f32[32,128]{1,0:T(8,128)S(1)} collective-permute-done((f32[32,128]{1,0:T(8,128)S(1)}, f32[32,128]{1,0:T(8,128)S(1)}, u32[]{:S(2)}, u32[]{:S(2)}) %collective-permute-start.7) | collective-permute-done | bytes 16416 | tf_op jit(solution)/shard_map/ppermute | solution.py:27
  (30 shorter events, 2.6 us)
Async XLA Ops:
  0.6 18.9 %copy-start.5 = (f32[16,128]{1,0:T(8,128)S(1)}, f32[16,128]{1,0:T(8,128)}, u32[]{:S(2)}) copy-start(f32[16,128]{1,0:T(8,128)} %param.13) | copy-start | bytes 24580
  0.6 18.9 %copy-start.4 = (f32[16,128]{1,0:T(8,128)S(1)}, f32[16,128]{1,0:T(8,128)}, u32[]{:S(2)}) copy-start(f32[16,128]{1,0:T(8,128)} %param.11) | copy-start | bytes 24580
  0.7 12.6 %collective-permute-start.1 = (f32[32,128]{1,0:T(8,128)}, f32[32,128]{1,0:T(8,128)S(1)}, u32[]{:S(2)}, u32[]{:S(2)}) collective-permute-start(f32[32,128]{1,0:T(8,128)} %param.12), channel_id=1, source_target_pairs={{1,0},{2,1},{3,2},{4,3},{5,4},{6,5},{7,6},{8,7},{9,8},{10,9},{11,1... | collective-permute-start | bytes 49160 | tf_op jit(solution)/shard_map/ppermute | solution.py:19
  5.0 8.2 %collective-permute-start = (f32[32,128]{1,0:T(8,128)}, f32[32,128]{1,0:T(8,128)S(1)}, u32[]{:S(2)}, u32[]{:S(2)}) collective-permute-start(f32[32,128]{1,0:T(8,128)} %param.12), channel_id=1, source_target_pairs={{0,1},{1,2},{2,3},{3,4},{4,5},{5,6},{6,7},{7,8},{8,9},{9,10},{10,1... | collective-permute-start | bytes 49160 | tf_op jit(solution)/shard_map/ppermute | solution.py:16
  11.6 18.6 %copy-start = (f32[64,128,128]{2,1,0:T(8,128)S(1)}, f32[64,128,128]{2,1,0:T(8,128)}, u32[]{:S(2)}) copy-start(f32[64,128,128]{2,1,0:T(8,128)} %param.15) | copy-start | bytes 12582916
  14.2 39.9 %copy-start.2 = (f32[32,128]{1,0:T(8,128)S(1)}, f32[32,128]{1,0:T(8,128)}, u32[]{:S(2)}) copy-start(f32[32,128]{1,0:T(8,128)} %param.12) | copy-start | bytes 49156
  14.2 39.9 %copy-start.3 = (f32[32,128]{1,0:T(8,128)S(1)}, f32[32,128]{1,0:T(8,128)}, u32[]{:S(2)}) copy-start(f32[32,128]{1,0:T(8,128)} %param.14) | copy-start | bytes 49156
  40.6 39.6 %copy-start.1 = (f32[64,128,128]{2,1,0:T(8,128)S(1)}, f32[64,128,128]{2,1,0:T(8,128)}, u32[]{:S(2)}) copy-start(f32[64,128,128]{2,1,0:T(8,128)} %param.15) | copy-start | bytes 12582916
  40.7 7.9 %collective-permute-start.2 = (f32[32,128]{1,0:T(8,128)S(1)}, f32[32,128]{1,0:T(8,128)S(1)}, u32[]{:S(2)}, u32[]{:S(2)}) collective-permute-start(f32[32,128]{1,0:T(8,128)S(1)} %get-tuple-element.8), channel_id=1, source_target_pairs={{1,0},{2,1},{3,2},{4,3},{5,4},{6,5},{7,6},{8,7},{9,8},{10,9},{11,1... | collective-permute-start | bytes 49160 | tf_op jit(solution)/shard_map/ppermute | solution.py:27
  46.6 7.4 %collective-permute-start.3 = (f32[32,128]{1,0:T(8,128)S(1)}, f32[32,128]{1,0:T(8,128)S(1)}, u32[]{:S(2)}, u32[]{:S(2)}) collective-permute-start(f32[32,128]{1,0:T(8,128)S(1)} %get-tuple-element.9), channel_id=1, source_target_pairs={{0,1},{1,2},{2,3},{3,4},{4,5},{5,6},{6,7},{7,8},{8,9},{9,10},{10,1... | collective-permute-start | bytes 49160 | tf_op jit(solution)/shard_map/ppermute | solution.py:27
  54.1 6.0 %collective-permute-start.5 = (f32[32,128]{1,0:T(8,128)S(1)}, f32[32,128]{1,0:T(8,128)S(1)}, u32[]{:S(2)}, u32[]{:S(2)}) collective-permute-start(f32[32,128]{1,0:T(8,128)S(1)} %fusion.37), channel_id=1, source_target_pairs={{1,0},{2,1},{3,2},{4,3},{5,4},{6,5},{7,6},{8,7},{9,8},{10,9},{11,1... | collective-permute-start | bytes 49160 | tf_op jit(solution)/shard_map/ppermute | solution.py:19
  56.0 7.4 %collective-permute-start.4 = (f32[32,128]{1,0:T(8,128)S(1)}, f32[32,128]{1,0:T(8,128)S(1)}, u32[]{:S(2)}, u32[]{:S(2)}) collective-permute-start(f32[32,128]{1,0:T(8,128)S(1)} %fusion.37), channel_id=1, source_target_pairs={{0,1},{1,2},{2,3},{3,4},{4,5},{5,6},{6,7},{7,8},{8,9},{9,10},{10,1... | collective-permute-start | bytes 49160 | tf_op jit(solution)/shard_map/ppermute | solution.py:16
  80.0 20.7 %copy-start.6 = (f32[16,128]{1,0:T(8,128)}, f32[16,128]{1,0:T(8,128)S(1)}, u32[]{:S(2)}) copy-start(f32[16,128]{1,0:T(8,128)S(1)} %get-tuple-element.35) | copy-start | bytes 24580
  90.7 5.9 %collective-permute-start.6 = (f32[32,128]{1,0:T(8,128)S(1)}, f32[32,128]{1,0:T(8,128)S(1)}, u32[]{:S(2)}, u32[]{:S(2)}) collective-permute-start(f32[32,128]{1,0:T(8,128)S(1)} %get-tuple-element.6), channel_id=1, source_target_pairs={{1,0},{2,1},{3,2},{4,3},{5,4},{6,5},{7,6},{8,7},{9,8},{10,9},{11,1... | collective-permute-start | bytes 49160 | tf_op jit(solution)/shard_map/ppermute | solution.py:27
  92.6 7.4 %collective-permute-start.7 = (f32[32,128]{1,0:T(8,128)S(1)}, f32[32,128]{1,0:T(8,128)S(1)}, u32[]{:S(2)}, u32[]{:S(2)}) collective-permute-start(f32[32,128]{1,0:T(8,128)S(1)} %get-tuple-element.7), channel_id=1, source_target_pairs={{0,1},{1,2},{2,3},{3,4},{4,5},{5,6},{6,7},{7,8},{8,9},{9,10},{10,1... | collective-permute-start | bytes 49160 | tf_op jit(solution)/shard_map/ppermute | solution.py:27
where the time goes:
time: 101 us
  matrix products  47.4 us (47%)
  starting transfers between devices  26.1 us (26%)
  waiting for transfers between devices  12.3 us (12%)
  blocking collectives  7.06 us (7%)
  local copies, waits for them, and re-layouts  3.31 us (3%)
  other arithmetic  2.99 us (3%)
  between operations  1.53 us (2%)
    dot_general x2, matrix products, body(): jnp.dot(col_select.T, backward, precision=lax.Precision.HIGHEST)  21.5 us
    ppermute x4, starting transfers between devices, shifted(): return lax.ppermute(block, axis, route)  13.7 us
    dot_general x2, matrix products, body(): jnp.einsum('nrc,nc->nr', tiles, primal_picked, precision=lax.Precision.HI...  13.2 us
    dot_general x2, matrix products, body(): jnp.einsum('nrc,nr->nc', tiles, dual_picked, precision=lax.Precision.HIGH...  10.6 us
    ppermute x4, waiting for transfers between devices, shifted(): return lax.ppermute(block, axis, route)  8.99 us
    psum x2, blocking collectives, body(): summed = lax.psum(window_terms, 'grp')  7.06 us
    ppermute x2, starting transfers between devices, with_halo(): lax.ppermute(lax.slice_in_dim(block, 0, width, axis=dim), axis, backward)  6.3 us
    ppermute x2, starting transfers between devices, with_halo(): lax.ppermute(lax.slice_in_dim(block, block.shape[dim] - width, None, axis...  6.03 us
  transfers between devices with their start and end apart: 8, of which 3 were waited for; matrix products, arithmetic and copies ran while one was open for 6% of the time, Pallas kernels for 0%

commit v1 on v0

--- a/solution.py
+++ b/solution.py
@@ -83,7 +83,7 @@
             * live_mask
         )
         window_terms = jnp.dot(row_select.T, forward, precision=lax.Precision.HIGHEST)
-        summed = lax.psum(window_terms, "grp")
+        summed = jnp.sum(lax.all_gather(window_terms, "grp"), axis=0)
         from_above = shifted(summed[:row_blocks], "tm", -1)
         from_below = shifted(summed[2 * row_blocks :], "tm", 1)
         image_slab = summed[row_blocks : 2 * row_blocks] + from_above + from_below

time: 101 us -> 98.1 us (0.971)
  blocking collectives: 7.06 us -> 3.75 us
    psum x2 -> x0, blocking collectives: 7.06 us -> none  [body(): summed = lax.psum(window_terms, 'grp')]
    all_gather x0 -> x2, blocking collectives: none -> 3.75 us  [body(): summed = jnp.sum(lax.all_gather(window_terms, 'grp'), axis=0)]
where the time goes in v1:
time: 98.1 us; the launch traced here: 97.4 us
  matrix products  47.4 us (48%)
  starting transfers between devices  26.1 us (27%)
  waiting for transfers between devices  12.3 us (13%)
  blocking collectives  3.75 us (4%)
  local copies, waits for them, and re-layouts  3.31 us (3%)
  other arithmetic  3 us (3%)
  between operations  1.52 us (2%)
    dot_general x2, matrix products, body(): jnp.dot(col_select.T, backward, precision=lax.Precision.HIGHEST)  21.5 us
    ppermute x4, starting transfers between devices, shifted(): return lax.ppermute(block, axis, route)  13.7 us
    dot_general x2, matrix products, body(): jnp.einsum('nrc,nc->nr', tiles, primal_picked, precision=lax.Precision.HI...  13.2 us
    dot_general x2, matrix products, body(): jnp.einsum('nrc,nr->nc', tiles, dual_picked, precision=lax.Precision.HIGH...  10.6 us
    ppermute x4, waiting for transfers between devices, shifted(): return lax.ppermute(block, axis, route)  8.99 us
    ppermute x2, starting transfers between devices, with_halo(): lax.ppermute(lax.slice_in_dim(block, 0, width, axis=dim), axis, backward)  6.3 us
    ppermute x2, starting transfers between devices, with_halo(): lax.ppermute(lax.slice_in_dim(block, block.shape[dim] - width, None, axis...  6.03 us
    all_gather x2, blocking collectives, body(): summed = jnp.sum(lax.all_gather(window_terms, 'grp'), axis=0)  3.75 us
  transfers between devices with their start and end apart: 8, of which 3 were waited for; matrix products, arithmetic and copies ran while one was open for 6% of the time, Pallas kernels for 0%

profile of v1, /device:TPU:16, one launch (start us, length us, event | category | flops | bytes accessed | tf_op | source)
XLA Modules:
  0.0 97.4 jit_solution(4004970547573323741)
XLA Ops:
  0.7 4.4 %collective-permute-start.1 = (f32[32,128]{1,0:T(8,128)}, f32[32,128]{1,0:T(8,128)S(1)}, u32[]{:S(2)}, u32[]{:S(2)}) collective-permute-start(f32[32,128]{1,0:T(8,128)} %param.12), channel_id=1, source_target_pairs={{1,0},{2,1},{3,2},{4,3},{5,4},{6,5},{7,6},{8,7},{9,8},{10,9},{11,1... | collective-permute-start | bytes 49160 | tf_op jit(solution)/shard_map/ppermute | solution.py:19
  5.0 1.9 %collective-permute-start = (f32[32,128]{1,0:T(8,128)}, f32[32,128]{1,0:T(8,128)S(1)}, u32[]{:S(2)}, u32[]{:S(2)}) collective-permute-start(f32[32,128]{1,0:T(8,128)} %param.12), channel_id=1, source_target_pairs={{0,1},{1,2},{2,3},{3,4},{4,5},{5,6},{6,7},{7,8},{8,9},{9,10},{10,1... | collective-permute-start | bytes 49160 | tf_op jit(solution)/shard_map/ppermute | solution.py:16
  7.6 1.6 %fusion.64 = (f32[1]{0:T(128)}, f32[1]{0:T(128)}, f32[1]{0:T(128)}, f32[1]{0:T(128)}, f32[1]{0:T(128)}, /*index=5*/f32[1]{0:T(128)}, f32[1]{0:T(128)}, f32[1]{0:T(128)}) fusion(f32[8]{0:T(128)} %param.20), kind=kLoop, calls=%fused_computation.84 | loop fusion | bytes 64 | tf_op jit(solution)/shard_map/slice | solution.py:59
  9.3 1.6 %fusion.63 = (f32[1]{0:T(128)}, f32[1]{0:T(128)}, f32[1]{0:T(128)}, f32[1]{0:T(128)}, f32[1]{0:T(128)}, /*index=5*/f32[1]{0:T(128)}, f32[1]{0:T(128)}, f32[1]{0:T(128)}) fusion(f32[8]{0:T(128)} %param.21), kind=kLoop, calls=%fused_computation.83 | loop fusion | bytes 64 | tf_op jit(solution)/shard_map/slice | solution.py:60
  11.6 0.8 broadcast_subtract_fusion.1
  12.4 0.8 broadcast_subtract_fusion
  13.3 0.9 fusion.8
  14.2 5.3 %fusion.65 = f32[64,1,128]{2,1,0:T(1,128)S(1)} fusion(f32[64,128,1]{1,2,0:T(1,128)S(1)} %bitcast.50, f32[64,128,128]{2,1,0:T(8,128)} %param.15), kind=kOutput, calls=%fused_computation.85 | convolution fusion | flops 12582912 | bytes 4259840 | tf_op jit(solution)/shard_map/nrc,nr->nc/dot_general | solution.py:73
  19.5 10.4 %fusion.7 = f32[16,128]{1,0:T(8,128)S(1)} fusion(f32[16,128]{1,0:T(8,128)S(1)} %copy-done.4, f32[16,128]{1,0:T(8,128)S(1)} %copy-done.5, f32[64,128]{1,0:T(8,128)S(1)} %bitcast.53, f32[64]{0:T(128)S(1)} %compare_convert_fusion, s32[64]{0:T(128)S(1)} %broadcast_subtract_fusion.1, pred[16,128]{1,0:T(8,128)(4,1)S(1)} %get-tuple-element.16, ...), kind=kOutput, calls=%fused_computation.9 | convolution fusion | flops 1625088 | bytes 74304 | tf_op jit(solution)/shard_map/dot_general | solution.py:76
  30.2 6.6 %fusion.66 = f32[64,1,128]{2,1,0:T(1,128)S(1)} fusion(f32[64,128,1]{1,2,0:T(1,128)S(1)} %bitcast.57, f32[64,128,128]{2,1,0:T(8,128)S(1)} %copy-done), kind=kOutput, calls=%fused_computation.86 | convolution fusion | flops 12582912 | bytes 4259840 | tf_op jit(solution)/shard_map/nrc,nc->nr/dot_general | solution.py:82
  37.1 1.9 %all-gather = f32[192,128]{1,0:T(8,128)S(1)} all-gather(f32[96,128]{1,0:T(8,128)S(1)} %fusion.23), channel_id=2, replica_groups=mesh['grp'=2,'tm'=16] {'grp'}, dimensions={0}, use_global_device_ids=true | all-gather | bytes 147456 | tf_op jit(solution)/shard_map/all_gather | solution.py:86
  39.0 6.0 %collective-permute-start.2 = (f32[32,128]{1,0:T(8,128)S(1)}, f32[32,128]{1,0:T(8,128)S(1)}, u32[]{:S(2)}, u32[]{:S(2)}) collective-permute-start(f32[32,128]{1,0:T(8,128)S(1)} %get-tuple-element.8), channel_id=1, source_target_pairs={{1,0},{2,1},{3,2},{4,3},{5,4},{6,5},{7,6},{8,7},{9,8},{10,9},{11,1... | collective-permute-start | bytes 49160 | tf_op jit(solution)/shard_map/ppermute | solution.py:27
  45.0 1.9 %collective-permute-start.3 = (f32[32,128]{1,0:T(8,128)S(1)}, f32[32,128]{1,0:T(8,128)S(1)}, u32[]{:S(2)}, u32[]{:S(2)}) collective-permute-start(f32[32,128]{1,0:T(8,128)S(1)} %get-tuple-element.9), channel_id=1, source_target_pairs={{0,1},{1,2},{2,3},{3,4},{4,5},{5,6},{6,7},{7,8},{8,9},{9,10},{10,1... | collective-permute-start | bytes 49160 | tf_op jit(solution)/shard_map/ppermute | solution.py:27
  46.9 5.5 %collective-permute-done.3 = f32[32,128]{1,0:T(8,128)S(1)} collective-permute-done((f32[32,128]{1,0:T(8,128)S(1)}, f32[32,128]{1,0:T(8,128)S(1)}, u32[]{:S(2)}, u32[]{:S(2)}) %collective-permute-start.3) | collective-permute-done | bytes 16416 | tf_op jit(solution)/shard_map/ppermute | solution.py:27
  52.4 1.9 %collective-permute-start.5 = (f32[32,128]{1,0:T(8,128)S(1)}, f32[32,128]{1,0:T(8,128)S(1)}, u32[]{:S(2)}, u32[]{:S(2)}) collective-permute-start(f32[32,128]{1,0:T(8,128)S(1)} %fusion.37), channel_id=1, source_target_pairs={{1,0},{2,1},{3,2},{4,3},{5,4},{6,5},{7,6},{8,7},{9,8},{10,9},{11,1... | collective-permute-start | bytes 49160 | tf_op jit(solution)/shard_map/ppermute | solution.py:19
  54.4 4.1 %collective-permute-start.4 = (f32[32,128]{1,0:T(8,128)S(1)}, f32[32,128]{1,0:T(8,128)S(1)}, u32[]{:S(2)}, u32[]{:S(2)}) collective-permute-start(f32[32,128]{1,0:T(8,128)S(1)} %fusion.37), channel_id=1, source_target_pairs={{0,1},{1,2},{2,3},{3,4},{4,5},{5,6},{6,7},{7,8},{8,9},{9,10},{10,1... | collective-permute-start | bytes 49160 | tf_op jit(solution)/shard_map/ppermute | solution.py:16
  58.5 3.3 %collective-permute-done.4 = f32[32,128]{1,0:T(8,128)S(1)} collective-permute-done((f32[32,128]{1,0:T(8,128)S(1)}, f32[32,128]{1,0:T(8,128)S(1)}, u32[]{:S(2)}, u32[]{:S(2)}) %collective-permute-start.4) | collective-permute-done | bytes 16416 | tf_op jit(solution)/shard_map/ppermute | solution.py:16
  62.0 5.3 %fusion.67 = f32[64,1,128]{2,1,0:T(1,128)S(1)} fusion(f32[64,128,1]{1,2,0:T(1,128)S(1)} %bitcast.51, f32[64,128,128]{2,1,0:T(8,128)} %param.15), kind=kOutput, calls=%fused_computation.87 | convolution fusion | flops 12582912 | bytes 4259840 | tf_op jit(solution)/shard_map/nrc,nr->nc/dot_general | solution.py:73
  67.3 11.1 %add_multiply_fusion.1 = (f32[16,128]{1,0:T(8,128)}, f32[16,128]{1,0:T(8,128)S(1)}) fusion(f32[16,128]{1,0:T(8,128)S(1)} %fusion.7, pred[16,128]{1,0:T(8,128)(4,1)S(1)} %get-tuple-element.16, pred[16,128]{1,0:T(8,128)(4,1)S(1)} %get-tuple-element.15, pred[16,128]{1,0:T(8,128)(4,1)S(1)} %get-tuple-element.14, pred[16,128]{1,0:T(8,128)(4,1)S(1)} %get-tuple-element.13, ...), kind=kOutput, calls=%fused_computation.57 | convolution fusion | flops 1629184 | bytes 82496 | tf_op jit(solution)/shard_map/dot_general | solution.py:76
  78.6 6.6 %fusion.68 = f32[64,1,128]{2,1,0:T(1,128)S(1)} fusion(f32[64,128,1]{1,2,0:T(1,128)S(1)} %bitcast.55, f32[64,128,128]{2,1,0:T(8,128)S(1)} %copy-done.1), kind=kOutput, calls=%fused_computation.88 | convolution fusion | flops 12582912 | bytes 4259840 | tf_op jit(solution)/shard_map/nrc,nc->nr/dot_general | solution.py:82
  85.5 1.9 %all-gather.1 = f32[192,128]{1,0:T(8,128)S(1)} all-gather(f32[96,128]{1,0:T(8,128)S(1)} %fusion.20), channel_id=3, replica_groups=mesh['grp'=2,'tm'=16] {'grp'}, dimensions={0}, use_global_device_ids=true | all-gather | bytes 147456 | tf_op jit(solution)/shard_map/all_gather | solution.py:86
  87.4 1.9 %collective-permute-start.6 = (f32[32,128]{1,0:T(8,128)S(1)}, f32[32,128]{1,0:T(8,128)S(1)}, u32[]{:S(2)}, u32[]{:S(2)}) collective-permute-start(f32[32,128]{1,0:T(8,128)S(1)} %get-tuple-element.6), channel_id=1, source_target_pairs={{1,0},{2,1},{3,2},{4,3},{5,4},{6,5},{7,6},{8,7},{9,8},{10,9},{11,1... | collective-permute-start | bytes 49160 | tf_op jit(solution)/shard_map/ppermute | solution.py:27
  89.3 3.9 %collective-permute-start.7 = (f32[32,128]{1,0:T(8,128)S(1)}, f32[32,128]{1,0:T(8,128)S(1)}, u32[]{:S(2)}, u32[]{:S(2)}) collective-permute-start(f32[32,128]{1,0:T(8,128)S(1)} %get-tuple-element.7), channel_id=1, source_target_pairs={{0,1},{1,2},{2,3},{3,4},{4,5},{5,6},{6,7},{7,8},{8,9},{9,10},{10,1... | collective-permute-start | bytes 49160 | tf_op jit(solution)/shard_map/ppermute | solution.py:27
  93.3 3.5 %collective-permute-done.7 = f32[32,128]{1,0:T(8,128)S(1)} collective-permute-done((f32[32,128]{1,0:T(8,128)S(1)}, f32[32,128]{1,0:T(8,128)S(1)}, u32[]{:S(2)}, u32[]{:S(2)}) %collective-permute-start.7) | collective-permute-done | bytes 16416 | tf_op jit(solution)/shard_map/ppermute | solution.py:27
  (32 shorter events, 2.7 us)
Async XLA Ops:
  0.6 18.9 %copy-start.5 = (f32[16,128]{1,0:T(8,128)S(1)}, f32[16,128]{1,0:T(8,128)}, u32[]{:S(2)}) copy-start(f32[16,128]{1,0:T(8,128)} %param.13) | copy-start | bytes 24580
  0.6 18.9 %copy-start.4 = (f32[16,128]{1,0:T(8,128)S(1)}, f32[16,128]{1,0:T(8,128)}, u32[]{:S(2)}) copy-start(f32[16,128]{1,0:T(8,128)} %param.11) | copy-start | bytes 24580
  0.7 12.6 %collective-permute-start.1 = (f32[32,128]{1,0:T(8,128)}, f32[32,128]{1,0:T(8,128)S(1)}, u32[]{:S(2)}, u32[]{:S(2)}) collective-permute-start(f32[32,128]{1,0:T(8,128)} %param.12), channel_id=1, source_target_pairs={{1,0},{2,1},{3,2},{4,3},{5,4},{6,5},{7,6},{8,7},{9,8},{10,9},{11,1... | collective-permute-start | bytes 49160 | tf_op jit(solution)/shard_map/ppermute | solution.py:19
  5.0 8.2 %collective-permute-start = (f32[32,128]{1,0:T(8,128)}, f32[32,128]{1,0:T(8,128)S(1)}, u32[]{:S(2)}, u32[]{:S(2)}) collective-permute-start(f32[32,128]{1,0:T(8,128)} %param.12), channel_id=1, source_target_pairs={{0,1},{1,2},{2,3},{3,4},{4,5},{5,6},{6,7},{7,8},{8,9},{9,10},{10,1... | collective-permute-start | bytes 49160 | tf_op jit(solution)/shard_map/ppermute | solution.py:16
  11.6 18.6 %copy-start = (f32[64,128,128]{2,1,0:T(8,128)S(1)}, f32[64,128,128]{2,1,0:T(8,128)}, u32[]{:S(2)}) copy-start(f32[64,128,128]{2,1,0:T(8,128)} %param.15) | copy-start | bytes 12582916
  14.2 38.2 %copy-start.2 = (f32[32,128]{1,0:T(8,128)S(1)}, f32[32,128]{1,0:T(8,128)}, u32[]{:S(2)}) copy-start(f32[32,128]{1,0:T(8,128)} %param.12) | copy-start | bytes 49156
  14.2 38.2 %copy-start.3 = (f32[32,128]{1,0:T(8,128)S(1)}, f32[32,128]{1,0:T(8,128)}, u32[]{:S(2)}) copy-start(f32[32,128]{1,0:T(8,128)} %param.14) | copy-start | bytes 49156
  39.0 39.6 %copy-start.1 = (f32[64,128,128]{2,1,0:T(8,128)S(1)}, f32[64,128,128]{2,1,0:T(8,128)}, u32[]{:S(2)}) copy-start(f32[64,128,128]{2,1,0:T(8,128)} %param.15) | copy-start | bytes 12582916
  39.0 7.9 %collective-permute-start.2 = (f32[32,128]{1,0:T(8,128)S(1)}, f32[32,128]{1,0:T(8,128)S(1)}, u32[]{:S(2)}, u32[]{:S(2)}) collective-permute-start(f32[32,128]{1,0:T(8,128)S(1)} %get-tuple-element.8), channel_id=1, source_target_pairs={{1,0},{2,1},{3,2},{4,3},{5,4},{6,5},{7,6},{8,7},{9,8},{10,9},{11,1... | collective-permute-start | bytes 49160 | tf_op jit(solution)/shard_map/ppermute | solution.py:27
  45.0 7.4 %collective-permute-start.3 = (f32[32,128]{1,0:T(8,128)S(1)}, f32[32,128]{1,0:T(8,128)S(1)}, u32[]{:S(2)}, u32[]{:S(2)}) collective-permute-start(f32[32,128]{1,0:T(8,128)S(1)} %get-tuple-element.9), channel_id=1, source_target_pairs={{0,1},{1,2},{2,3},{3,4},{4,5},{5,6},{6,7},{7,8},{8,9},{9,10},{10,1... | collective-permute-start | bytes 49160 | tf_op jit(solution)/shard_map/ppermute | solution.py:27
  52.4 6.0 %collective-permute-start.5 = (f32[32,128]{1,0:T(8,128)S(1)}, f32[32,128]{1,0:T(8,128)S(1)}, u32[]{:S(2)}, u32[]{:S(2)}) collective-permute-start(f32[32,128]{1,0:T(8,128)S(1)} %fusion.37), channel_id=1, source_target_pairs={{1,0},{2,1},{3,2},{4,3},{5,4},{6,5},{7,6},{8,7},{9,8},{10,9},{11,1... | collective-permute-start | bytes 49160 | tf_op jit(solution)/shard_map/ppermute | solution.py:19
  54.4 7.4 %collective-permute-start.4 = (f32[32,128]{1,0:T(8,128)S(1)}, f32[32,128]{1,0:T(8,128)S(1)}, u32[]{:S(2)}, u32[]{:S(2)}) collective-permute-start(f32[32,128]{1,0:T(8,128)S(1)} %fusion.37), channel_id=1, source_target_pairs={{0,1},{1,2},{2,3},{3,4},{4,5},{5,6},{6,7},{7,8},{8,9},{9,10},{10,1... | collective-permute-start | bytes 49160 | tf_op jit(solution)/shard_map/ppermute | solution.py:16
  78.4 19.0 %copy-start.6 = (f32[16,128]{1,0:T(8,128)}, f32[16,128]{1,0:T(8,128)S(1)}, u32[]{:S(2)}) copy-start(f32[16,128]{1,0:T(8,128)S(1)} %get-tuple-element.35) | copy-start | bytes 24580
  87.4 5.9 %collective-permute-start.6 = (f32[32,128]{1,0:T(8,128)S(1)}, f32[32,128]{1,0:T(8,128)S(1)}, u32[]{:S(2)}, u32[]{:S(2)}) collective-permute-start(f32[32,128]{1,0:T(8,128)S(1)} %get-tuple-element.6), channel_id=1, source_target_pairs={{1,0},{2,1},{3,2},{4,3},{5,4},{6,5},{7,6},{8,7},{9,8},{10,9},{11,1... | collective-permute-start | bytes 49160 | tf_op jit(solution)/shard_map/ppermute | solution.py:27
  89.3 7.4 %collective-permute-start.7 = (f32[32,128]{1,0:T(8,128)S(1)}, f32[32,128]{1,0:T(8,128)S(1)}, u32[]{:S(2)}, u32[]{:S(2)}) collective-permute-start(f32[32,128]{1,0:T(8,128)S(1)} %get-tuple-element.7), channel_id=1, source_target_pairs={{0,1},{1,2},{2,3},{3,4},{4,5},{5,6},{6,7},{7,8},{8,9},{9,10},{10,1... | collective-permute-start | bytes 49160 | tf_op jit(solution)/shard_map/ppermute | solution.py:27
